TPU v7x, 32 devices: a whole 2x2x4 slice. The times are simulated.
32 devices in a mesh: dp: 4 (over x, core), ctx: 4 (over z), tensor: 2 (over y).
Axes of the slice: x: 2, y: 2, z: 4, core: 2. Of those that a mesh axis runs over, the one named last changes fastest.
Arguments:
- query: bfloat16 [4, 512, 32, 128], P('dp', 'ctx', 'tensor'), may hold values from -200 to 200
- key_value: bfloat16 [2, 4, 512, 2, 128], P(None, 'dp', 'ctx'), may hold values from -7 to 7
- grad_out: bfloat16 [4, 512, 32, 128], P('dp', 'ctx', 'tensor'), may hold values from -6 to 6
- doc_lengths: int32 [4, 16], P('dp'), may hold values from 1 to 80, 512 in all within a row
- stretch_order: int32 [4, 4], P('dp'), may hold values from 0 to 3, each once within a row
- loss_mask: int32 [4, 512], P('dp', 'ctx'), may hold values from 0 to 1
Outputs:
- attended: bfloat16 [4, 512, 32, 128], P('dp', 'ctx', 'tensor')
- grad_query: bfloat16 [4, 512, 32, 128], P('dp', 'ctx', 'tensor')
- grad_key_value: bfloat16 [2, 4, 512, 2, 128], P(None, 'dp', 'ctx')
Inputs may be any that keep to these rules, and one draw needn't show every extreme that they name: `doc_lengths`: each row sums to 512 and its largest entry is 80. `stretch_order`: each row names every block index of its sequence once.
All inputs are finite; a program needn't handle non-finite values.
Results may differ from a plain program's by a relative error of at most 0.03.
Values may be sent and summed in bfloat16 or wider, within the bound.
A program may use at most 64 MiB of HBM per device.

v0:
```python
import math

import jax
import jax.numpy as jnp
from jax import lax
from jax.sharding import PartitionSpec as P

FLOOR_SCORE = -1e30


def document_ids(bounds, places):
    return jnp.sum((bounds[None, :] <= places[:, None]).astype(jnp.int32), axis=1)


def local(query, key_value, grad_out, doc_lengths, stretch_order, loss_mask):
    shard_rows = query.shape[1]
    local_heads = query.shape[2]
    head_width = query.shape[3]
    ctx_devices = lax.axis_size("ctx")
    length = shard_rows * ctx_devices
    longest = length * 5 // 32
    window = (longest - 1 + shard_rows - 1) // shard_rows
    slot_count = window + 1
    factor = 1.0 / math.sqrt(head_width)
    counted = lax.psum(jnp.sum(loss_mask.astype(jnp.float32)), ("dp", "ctx"))
    weight = lax.axis_size("dp") * query.shape[0] * length / jnp.maximum(counted, 1.0)
    own_head = lax.axis_index("tensor")
    own_pair = lax.dynamic_index_in_dim(key_value[:, 0], own_head, 2, keepdims=False)
    fetched = lax.all_gather(own_pair, "ctx", axis=1, tiled=True)
    keys_all = fetched[0]
    values_all = fetched[1]
    order_row = stretch_order[0]
    offsets = jnp.arange(shard_rows, dtype=jnp.int32)
    stretch_ids = jnp.arange(ctx_devices, dtype=jnp.int32)
    own_stretch = order_row[lax.axis_index("ctx")]
    query_places = own_stretch * shard_rows + offsets
    bounds = jnp.cumsum(doc_lengths[0])
    query_docs = document_ids(bounds, query_places)
    queries = jnp.transpose(query[0], (1, 0, 2))
    scaled = (
        grad_out[0].astype(jnp.float32) * loss_mask[0][:, None, None].astype(jnp.float32) * weight
    ).astype(jnp.bfloat16)
    upstream = jnp.transpose(scaled, (1, 0, 2))
    rows_shape = (local_heads, shard_rows)

    def block_view(slot_index):
        target = own_stretch - window + slot_index
        holder = jnp.sum(jnp.where(order_row == target, stretch_ids, 0))
        first_row = holder * shard_rows
        block_keys = lax.dynamic_slice_in_dim(keys_all, first_row, shard_rows, 0)
        block_values = lax.dynamic_slice_in_dim(values_all, first_row, shard_rows, 0)
        block_places = target * shard_rows + offsets
        block_docs = document_ids(bounds, block_places)
        visible = (
            (target >= 0)
            & (query_docs[:, None] == block_docs[None, :])
            & (block_places[None, :] <= query_places[:, None])
        )
        return (first_row, block_keys, block_values, visible)

    def scores_of(block_keys, visible):
        scores = (
            jnp.einsum("htd,kd->htk", queries, block_keys, preferred_element_type=jnp.float32)
            * factor
        )
        return jnp.where(visible[None], scores, FLOOR_SCORE)

    def forward_step(slot_index, carried):
        first_row, block_keys, block_values, visible = block_view(slot_index)

        def forward_compute(current):
            highest, row_total, summed = current
            scores = scores_of(block_keys, visible)
            raised = jnp.maximum(highest, jnp.max(scores, axis=2))
            rescale = jnp.exp(highest - raised)
            exponent = jnp.where(visible[None], jnp.exp(scores - raised[..., None]), 0.0)
            summed = summed * rescale[..., None] + jnp.einsum(
                "htk,kd->htd",
                exponent.astype(jnp.bfloat16),
                block_values,
                preferred_element_type=jnp.float32,
            )
            return (raised, row_total * rescale + jnp.sum(exponent, axis=2), summed)

        return lax.cond(jnp.any(visible), forward_compute, lambda current: current, carried)

    start_state = (
        jnp.full(rows_shape, FLOOR_SCORE, jnp.float32),
        jnp.zeros(rows_shape, jnp.float32),
        jnp.zeros((local_heads, shard_rows, head_width), jnp.float32),
    )
    highest, row_total, summed = lax.fori_loop(0, slot_count, forward_step, start_state)
    attended_heads = (summed / row_total[..., None]).astype(jnp.bfloat16)
    row_delta = jnp.sum(upstream.astype(jnp.float32) * attended_heads.astype(jnp.float32), axis=2)

    def backward_block(block_keys, block_values, visible):
        scores = scores_of(block_keys, visible)
        probabilities = (
            jnp.where(visible[None], jnp.exp(scores - highest[..., None]), 0.0)
            / row_total[..., None]
        )
        prob_grad = jnp.einsum(
            "htd,kd->htk", upstream, block_values, preferred_element_type=jnp.float32
        )
        score_grad = (probabilities * (prob_grad - row_delta[..., None])).astype(jnp.bfloat16)
        return (probabilities.astype(jnp.bfloat16), score_grad)

    def key_value_terms(probs_low, score_grad):
        key_part = (
            jnp.einsum("htk,htd->kd", score_grad, queries, preferred_element_type=jnp.float32)
            * factor
        )
        value_part = jnp.einsum(
            "htk,htd->kd", probs_low, upstream, preferred_element_type=jnp.float32
        )
        return jnp.stack([key_part, value_part], axis=1)

    empty_rows = jnp.zeros((local_heads, shard_rows, head_width), jnp.float32)

    def grad_step(slot_index, carried):
        first_row, block_keys, block_values, visible = block_view(slot_index)

        def grad_compute(current):
            grad_rows, partial_value = current
            probs_low, score_grad = backward_block(block_keys, block_values, visible)
            grad_rows = grad_rows + jnp.einsum(
                "htk,kd->htd", score_grad, block_keys, preferred_element_type=jnp.float32
            )
            block_terms = key_value_terms(probs_low, score_grad)
            partial_value = lax.dynamic_update_slice_in_dim(
                partial_value, block_terms, first_row, 0
            )
            return (grad_rows, partial_value)

        return lax.cond(jnp.any(visible), grad_compute, lambda current: current, carried)

    grad_rows, partial_value = lax.fori_loop(
        0, slot_count, grad_step, (empty_rows, jnp.zeros((length, 2, head_width), jnp.float32))
    )
    reduced = lax.psum_scatter(
        partial_value.astype(jnp.bfloat16), "ctx", scatter_dimension=0, tiled=True
    )
    grad_query = jnp.transpose((grad_rows * factor).astype(jnp.bfloat16), (1, 0, 2))[None]
    collected = lax.all_gather(reduced[:, :, None, :], "tensor", axis=2, tiled=True)
    grad_key_value = jnp.transpose(collected, (1, 0, 2, 3))[:, None]
    attended = jnp.transpose(attended_heads, (1, 0, 2))[None]
    return (attended, grad_query, grad_key_value)


def solution(mesh):
    placed = (
        P("dp", "ctx", "tensor", None),
        P(None, "dp", "ctx", None, None),
        P("dp", "ctx", "tensor", None),
        P("dp", None),
        P("dp", None),
        P("dp", "ctx"),
    )
    return jax.shard_map(
        local,
        mesh=mesh,
        in_specs=placed,
        out_specs=(
            P("dp", "ctx", "tensor", None),
            P("dp", "ctx", "tensor", None),
            P(None, "dp", "ctx", None, None),
        ),
        check_vma=False,
    )
```

profile of v0, /device:TPU:0, one launch (start us, length us, event | category | flops | bytes accessed | tf_op | source)
XLA Modules:
  0.0 116.0 jit_solution(1018360595519967742)
XLA Ops:
  7.2 0.7 copy-done.6
  8.5 35.8 %psum.7 = f32[]{:T(128)} all-reduce(f32[]{:T(128)} %convert_reduce_fusion.3), channel_id=1, replica_groups=mesh['dp'=4,'ctx'=4,'tensor'=2] {'dp','ctx'}, use_global_device_ids=true, to_apply=%region_12.13 | all-reduce | flops 1 | bytes 8 | tf_op jit(solution)/shard_map/psum | solution.py:25
  45.0 0.7 fusion.61
  47.4 14.0 %all-gather = bf16[2,1,512,1,128]{4,2,3,1,0:T(8,128)(2,1)S(1)} all-gather(bf16[2,1,128,1,128]{4,2,3,1,0:T(8,128)(2,1)S(1)} %copy.49), channel_id=2, replica_groups=mesh['dp'=4,'ctx'=4,'tensor'=2] {'ctx'}, dimensions={2}, use_global_device_ids=true | all-gather | bytes 327680 | tf_op jit(solution)/shard_map/all_gather | solution.py:29
  61.8 9.6 %while.38 = (s32[]{:T(128)}, f32[16,128]{1,0:T(8,128)S(1)}, f32[16,128]{1,0:T(8,128)S(1)}, f32[16,128,128]{2,1,0:T(8,128)S(1)}, s32[]{:T(128)}, /*index=5*/s32[1...) while((s32[]{:T(128)}, f32[16,128]{1,0:T(8,128)S(1)}, ...), condition=%wide.region_10.11_spmd.clone, body=%wide.region_2.10_spmd.clone.sunk | while | flops 137193616 | bytes 6033915 | solution.py:92
  62.7 0.8 fusion.71
  64.0 2.5 %conditional.6 = ((f32[16,128]{1,0:T(8,128)S(1)}, f32[16,128]{1,0:T(8,128)S(1)}, f32[16,128,128]{2,1,0:T(8,128)S(1)})) conditional(s32[]{:T(128)} %convert_element_type.138, (f32[16,128]{1,0:T(8,128)S(1)}, f32[16,128]{1,0:T(8,128)S(1)}, f32[16,128,128]{2,1,0:T(8,128)S(1)}) %tuple.138, (pred[128,128]{0,1:T(8,128)(4,1)S(1)}, s32[]{:T(128)}, ...), branch_computations={%region_5.5_spmd, %region_6.9_spmd} | conditional | flops 137105424 | bytes 6013054 | solution.py:85
  64.0 0.7 fusion.24
  65.9 0.7 convolution_add_fusion
  67.4 0.8 fusion.71
  68.8 2.5 %conditional.6 = ((f32[16,128]{1,0:T(8,128)S(1)}, f32[16,128]{1,0:T(8,128)S(1)}, f32[16,128,128]{2,1,0:T(8,128)S(1)})) conditional(s32[]{:T(128)} %convert_element_type.138, (f32[16,128]{1,0:T(8,128)S(1)}, f32[16,128]{1,0:T(8,128)S(1)}, f32[16,128,128]{2,1,0:T(8,128)S(1)}) %tuple.138, (pred[128,128]{0,1:T(8,128)(4,1)S(1)}, s32[]{:T(128)}, ...), branch_computations={%region_5.5_spmd, %region_6.9_spmd} | conditional | flops 137105424 | bytes 6013054 | solution.py:85
  68.8 0.7 fusion.24
  70.6 0.7 convolution_add_fusion
  72.1 1.7 %multiply_reduce_fusion = (f32[16,128]{0,1:T(8,128)S(1)}, bf16[16,128,128]{2,0,1:T(8,128)(2,1)S(1)}, bf16[16,128,128]{2,0,1:T(8,128)(2,1)}) fusion(f32[]{:T(128)S(6)} %div.29, f32[128]{0:T(128)S(1)} %convert_bitcast_fusion, bf16[1,128,16,128]{3,2,1,0:T(8,128)(2,1)S(1)} %copy-done.2, f32[16,128]{0,1:T(8,128)S(1)} %copy.42, ...), kind=kLoop, calls=%fused_computation.71 | loop fusion | flops 2619392 | bytes 2638340 | tf_op jit(solution)/shard_map/reduce_sum | solution.py:94
  74.2 10.5 %while.39 = (s32[]{:T(128)}, f32[16,128,128]{2,1,0:T(8,128)S(1)}, bf16[512,2,128]{2,0,1:T(8,128)(2,1)S(1)}, s32[]{:T(128)}, s32[128]{0:T(128)S(1)}, /*index=5*/s...) while((s32[]{:T(128)}, f32[16,128,128]{2,1,0:T(8,128)S(1)}, ...), condition=%wide.region_20.21_spmd.clone, body=%wide.region_14.20_spmd.clone.sunk | while | flops 338417792 | bytes 9269795 | solution.py:137
  75.0 0.7 fusion.72
  76.4 3.1 %conditional.7 = ((f32[16,128,128]{2,1,0:T(8,128)S(1)}, bf16[512,2,128]{2,0,1:T(8,128)(2,1)S(1)})) conditional(s32[]{:T(128)} %convert_element_type.140, (f32[16,128,128]{2,1,0:T(8,128)S(1)}, bf16[512,2,128]{2,0,1:T(8,128)(2,1)S(1)}) %tuple.143, (pred[128,128]{0,1:T(8,128)(4,1)S(1)}, s32[]{:T(128)}, s32[4]{0:T(128)S(1)}, s32[4]{0:T(128)S(1)}, ...), branch_computations={%region_17.17_spmd, %region_18.19_spmd} | conditional | flops 338329600 | bytes 9248894 | solution.py:135
  80.3 0.7 fusion.72
  81.7 3.1 %conditional.7 = ((f32[16,128,128]{2,1,0:T(8,128)S(1)}, bf16[512,2,128]{2,0,1:T(8,128)(2,1)S(1)})) conditional(s32[]{:T(128)} %convert_element_type.140, (f32[16,128,128]{2,1,0:T(8,128)S(1)}, bf16[512,2,128]{2,0,1:T(8,128)(2,1)S(1)}) %tuple.143, (pred[128,128]{0,1:T(8,128)(4,1)S(1)}, s32[]{:T(128)}, s32[4]{0:T(128)S(1)}, s32[4]{0:T(128)S(1)}, ...), branch_computations={%region_17.17_spmd, %region_18.19_spmd} | conditional | flops 338329600 | bytes 9248894 | solution.py:135
  84.8 0.7 copy-done.1
  85.5 1.5 %fusion.54 = bf16[1,128,16,128]{3,2,1,0:T(8,128)(2,1)} fusion(f32[16,128,128]{2,1,0:T(8,128)S(1)} %get-tuple-element.1054), kind=kLoop, calls=%fused_computation.72 | loop fusion | flops 524288 | bytes 1572864 | tf_op jit(solution)/shard_map/broadcast_in_dim | solution.py:143
  86.9 16.3 %reduce-scatter.2.cloned.1.call-done = bf16[128,2,128]{2,0,1:T(8,128)(2,1)} async-done(((bf16[512,2,128]{2,0,1:T(8,128)(2,1)}), bf16[128,2,128]{2,0,1:T(8,128)(2,1)}) %reduce-scatter.2.cloned.1.call-update) | async-done | bytes 65552 | tf_op jit(solution)/shard_map/reduce_scatter | solution.py:140
  103.3 5.2 %all-gather.1 = bf16[128,2,256]{2,0,1:T(8,128)(2,1)S(1)} all-gather(bf16[128,2,128]{2,0,1:T(8,128)(2,1)} %reduce-scatter.2.cloned.1.call-done), channel_id=3, replica_groups=mesh['dp'=4,'ctx'=4,'tensor'=2] {'tensor'}, dimensions={2}, use_global_device_ids=true | all-gather | bytes 196608 | tf_op jit(solution)/shard_map/all_gather | solution.py:144
  108.5 0.7 reshape.96
  (69 shorter events, 9.3 us)
Async XLA Ops:
  7.2 40.0 %copy-start = (bf16[2,1,128,2,128]{4,3,2,1,0:T(2,128)(2,1)S(1)}, bf16[2,1,128,2,128]{4,3,2,1,0:T(2,128)(2,1)}, u32[]{:S(2)}) copy-start(bf16[2,1,128,2,128]{4,3,2,1,0:T(2,128)(2,1)} %param.15) | copy-start | bytes 393220
  7.2 96.1 %reduce-scatter.2.cloned.1.call-start = ((), (), s32[]{:S(2)}) async-start(), calls=%async_computation.1 | async-start | bytes 327680 | tf_op jit(solution)/shard_map/reduce_scatter | solution.py:140
  7.2 0.7 copy-start.6
  44.3 0.7 copy-start.4
  46.3 0.7 copy-start.5
  47.3 14.1 %copy-start.3 = (bf16[1,128,16,128]{3,2,1,0:T(8,128)(2,1)S(1)}, bf16[1,128,16,128]{3,2,1,0:T(8,128)(2,1)}, u32[]{:S(2)}) copy-start(bf16[1,128,16,128]{3,2,1,0:T(8,128)(2,1)} %param.14) | copy-start | bytes 1572868
  61.8 10.4 %copy-start.2 = (bf16[1,128,16,128]{3,2,1,0:T(8,128)(2,1)S(1)}, bf16[1,128,16,128]{3,2,1,0:T(8,128)(2,1)}, u32[]{:S(2)}) copy-start(bf16[1,128,16,128]{3,2,1,0:T(8,128)(2,1)} %param.16) | copy-start | bytes 1572868
  84.8 0.7 copy-start.1
Sparse Core Ops, SparseCore 0:
  85.6 17.6 reduce-scatter.1
where the time goes:
time: 116 us
  blocking collectives  55 us (47%)
  waiting for transfers between devices  16.4 us (14%)
  between operations  15.5 us (13%)
  other arithmetic  11.2 us (10%)
  loops' own time  8.29 us (7%)
  matrix products  5.35 us (5%)
  local copies, waits for them, and re-layouts  4.3 us (4%)
    psum x1, blocking collectives, local(): counted = lax.psum(jnp.sum(loss_mask.astype(jnp.float32)), ('dp', 'ctx'))  35.8 us
    reduce_scatter x1, waiting for transfers between devices, local(): lax.psum_scatter(partial_value.astype(jnp.bfloat16), 'ctx', scatter_dimen...  16.3 us
    all_gather x1, blocking collectives, local(): fetched = lax.all_gather(own_pair, 'ctx', axis=1, tiled=True)  14 us
    all_gather x1, blocking collectives, local(): lax.all_gather(reduced[:, :, None, :], 'tensor', axis=2, tiled=True)  5.16 us
    unnamed x18, local copies, waits for them, and re-layouts  3.04 us
    another operation x1, loops' own time, local(): lax.fori_loop(0, slot_count, grad_step, (empty_rows, jnp.zeros((length, 2...  2.77 us
    another operation x1, loops' own time, local(): lax.fori_loop(0, slot_count, forward_step, start_state)  2.75 us
    reduce_sum x4, other arithmetic, block_view(): holder = jnp.sum(jnp.where(order_row == target, stretch_ids, 0))  2.59 us
  transfers between devices with their start and end apart: 1, of which 1 were waited for; matrix products, arithmetic and copies ran while one was open for 1% of the time, Pallas kernels for 0%

commit v1 on v0

v1 whole, which is shorter than its diff:
```python
import functools
import math

import jax
import jax.numpy as jnp
from jax import lax
from jax.experimental import pallas as pl
from jax.experimental.pallas import tpu as pltpu
from jax.sharding import PartitionSpec as P

HIDDEN = -1e30
CHUNK_TOKENS = 16
F32 = jnp.float32
BF16 = jnp.bfloat16


def dot(left, right):
    return lax.dot_general(left, right, (((1,), (0,)), ((), ())), preferred_element_type=F32)


def dot_t(left, right):
    return lax.dot_general(left, right, (((1,), (1,)), ((), ())), preferred_element_type=F32)


def dot_l(left, right):
    return lax.dot_general(left, right, (((0,), (0,)), ((), ())), preferred_element_type=F32)


def kernel(
    sizes,
    q_hbm, kv_hbm, g_hbm, doc_hbm, order_hbm, mask_hbm,
    att_hbm, dq_hbm, dkv_hbm,
    q_ref, kv_ref, g_ref, doc_ref, order_ref, mask_ref,
    att_ref, dq_ref, dkv_ref,
    kvs, counts, dcounts, pieces, staged, landed, heads_ref,
    e_ref, po_ref, dpo_ref, atto_ref, pmo_ref, dso_ref, pp_ref, pmp_ref, dsp_ref,
    local_sem, kv_send, kv_recv, count_send, count_recv, dcount_send, dcount_recv,
    grad_send, grad_recv, head_send, head_recv,
):
    n, nd, nt, rows, heads, width, window, tail, docs, part_chunks, weight_top = sizes
    me = lax.axis_index("ctx")
    my_dp = lax.axis_index("dp")
    my_head = lax.axis_index("tensor")
    chunk = CHUNK_TOKENS * heads
    chunks = rows // CHUNK_TOKENS
    skip = rows - tail
    factor = 1.0 / math.sqrt(width)
    steep = factor * math.log2(math.e)

    barrier = pltpu.get_barrier_semaphore()
    for axis, mine, count in (("ctx", me, n), ("dp", my_dp, nd), ("tensor", my_head, nt)):
        for step in range(1, count):
            pl.semaphore_signal(
                barrier,
                inc=1,
                device_id={axis: lax.rem(mine + step, count)},
                device_id_type=pl.DeviceIdType.MESH,
            )

    loads = [
        pltpu.make_async_copy(source, target, local_sem.at[i])
        for i, (source, target) in enumerate(
            (
                (kv_hbm, kv_ref),
                (mask_hbm, mask_ref),
                (doc_hbm, doc_ref),
                (order_hbm, order_ref),
                (q_hbm, q_ref),
                (g_hbm, g_ref),
            )
        )
    ]
    for load in loads:
        load.start()

    def remote(source, target, send, recv, axis, mine, count, step):
        return pltpu.make_async_remote_copy(
            src_ref=source,
            dst_ref=target,
            send_sem=send.at[step],
            recv_sem=recv.at[step],
            device_id={axis: lax.rem(mine + step, count)},
            device_id_type=pl.DeviceIdType.MESH,
        )

    gap = lax.broadcasted_iota(jnp.int32, (chunk, rows), 0) - heads * lax.broadcasted_iota(
        jnp.int32, (chunk, rows), 1
    )
    for c in range(chunks):
        moved = gap + c * chunk
        e_ref[c] = jnp.where((moved >= 0) & (moved < heads), 1.0, 0.0).astype(BF16)
    pick = (
        lax.broadcasted_iota(jnp.int32, (rows, rows * nt), 1)
        - nt * lax.broadcasted_iota(jnp.int32, (rows, rows * nt), 0)
    )
    own_pick = jnp.where(pick == my_head, 1.0, 0.0).astype(BF16)

    loads[0].wait()
    k_own = dot(own_pick, kv_ref[0]).astype(BF16)
    v_own = dot(own_pick, kv_ref[1]).astype(BF16)
    kvs[me, 0] = k_own[skip:]
    kvs[me, 1] = v_own[skip:]
    loads[1].wait()
    counts[me] = mask_ref[...]
    pl.semaphore_wait(barrier, n + nd + nt - 3)
    kv_copies = [
        remote(kvs.at[me], kvs.at[me], kv_send, kv_recv, "ctx", me, n, step)
        for step in range(1, n)
    ]
    for copy in kv_copies:
        copy.start()
    count_copies = [
        remote(counts.at[me], counts.at[me], count_send, count_recv, "ctx", me, n, step)
        for step in range(1, n)
    ]
    for copy in count_copies:
        copy.start()

    loads[2].wait()
    loads[3].wait()
    own = order_ref[0, me]
    token_row = lax.broadcasted_iota(jnp.int32, (1, rows), 1)
    place_row = own * rows + token_row
    start_row = jnp.zeros((1, rows), jnp.int32)
    bound = jnp.int32(0)
    for j in range(docs):
        bound = bound + doc_ref[0, j]
        start_row = jnp.where(bound <= place_row, bound, start_row)
    key_rows = lax.broadcasted_iota(jnp.int32, (rows, rows), 0)

    def bias_of(target):
        key_places = target * rows + key_rows
        seen = (key_places >= start_row) & (key_places <= place_row)
        return jnp.where(seen, 0.0, HIDDEN).astype(BF16)

    def flipped(block):
        return jnp.transpose(block.astype(F32)).astype(BF16)

    wide_own = jnp.concatenate([k_own, bias_of(own)], axis=1)
    kt_own = flipped(k_own)
    vt_own = flipped(v_own)
    mask_rows = jnp.broadcast_to(mask_ref[...].astype(F32), (8, rows)).astype(BF16)

    def cols(c):
        return pl.ds(c * chunk, chunk)

    def wide_queries(c):
        return jnp.concatenate([q_ref[cols(c), :], e_ref[c]], axis=1)

    loads[4].wait()
    loads[5].wait()
    top, total, drift, kept = [], [], [], []

    def close_own(c, gain, delta):
        masked = po_ref[:, cols(c)] * gain
        pmo_ref[:, cols(c)] = masked.astype(BF16)
        dso_ref[:, cols(c)] = (masked * (dpo_ref[:, cols(c)] - delta)).astype(BF16)

    for c in range(chunks):
        scores = dot_t(wide_own, wide_queries(c))
        grads = dot_t(v_own, g_ref[cols(c), :])
        highest = jnp.max(scores, axis=0, keepdims=True)
        raised = jnp.exp2((scores - highest) * steep)
        summed = jnp.sum(raised, axis=0, keepdims=True)
        drifted = jnp.sum(raised * grads, axis=0, keepdims=True)
        top.append(highest)
        total.append(summed)
        drift.append(drifted)
        kept.append(dot_t(mask_rows, e_ref[c])[0:1])
        po_ref[:, cols(c)] = raised
        dpo_ref[:, cols(c)] = grads
        own_part = dot(vt_own, raised.astype(BF16))
        if c < part_chunks:
            atto_ref[:, cols(c)] = own_part
        else:
            inverse = 1.0 / summed
            close_own(c, kept[c] * inverse, drifted * inverse)
            att_ref[cols(c), :] = jnp.transpose(own_part * inverse).astype(BF16)

    for copy in kv_copies:
        copy.wait()
    for copy in count_copies:
        copy.wait()
    dcounts[my_dp] = jnp.sum(counts[...], axis=0)
    dcount_copies = [
        remote(dcounts.at[my_dp], dcounts.at[my_dp], dcount_send, dcount_recv, "dp", my_dp, nd, step)
        for step in range(1, nd)
    ]
    for copy in dcount_copies:
        copy.start()
    targets, wide, values, kts, vts = [], [], [], [], []
    for w in range(window):
        target = own - 1 - w
        holder = jnp.int32(0)
        for j in range(n):
            holder = holder + jnp.where(order_ref[0, j] == target, j, 0)
        pair = kvs[holder]
        empty = jnp.zeros((skip, width), BF16)
        block_k = jnp.concatenate([empty, pair[0]], axis=0) if skip else pair[0]
        block_v = jnp.concatenate([empty, pair[1]], axis=0) if skip else pair[1]
        targets.append(target)
        wide.append(jnp.concatenate([block_k, bias_of(target)], axis=1))
        values.append(block_v)
        kts.append(flipped(block_k))
        vts.append(flipped(block_v))

    gains, deltas, inverses, fades = [], [], [], []
    for c in range(part_chunks):
        queries = wide_queries(c)
        scores = [dot_t(wide[w], queries) for w in range(window)]
        grads = [dot_t(values[w], g_ref[cols(c), :]) for w in range(window)]
        highest = top[c]
        for w in range(window):
            highest = jnp.maximum(highest, jnp.max(scores[w], axis=0, keepdims=True))
        fade = jnp.exp2((top[c] - highest) * steep)
        summed = total[c] * fade
        drifted = drift[c] * fade
        raised = []
        for w in range(window):
            part = jnp.exp2((scores[w] - highest) * steep)
            summed = summed + jnp.sum(part, axis=0, keepdims=True)
            drifted = drifted + jnp.sum(part * grads[w], axis=0, keepdims=True)
            pp_ref[w, :, cols(c)] = part.astype(BF16)
            raised.append(part)
        inverse = 1.0 / summed
        delta = drifted * inverse
        gain = kept[c] * inverse
        for w in range(window):
            masked = raised[w] * gain
            pmp_ref[w, :, cols(c)] = masked.astype(BF16)
            dsp_ref[w, :, cols(c)] = (masked * (grads[w] - delta)).astype(BF16)
        gains.append(gain * fade)
        deltas.append(delta)
        inverses.append(inverse)
        fades.append(fade)

    part_rows = part_chunks * chunk
    for w in range(window):
        pieces[w, 0] = (dot(dsp_ref[w], q_ref[:part_rows, :])[skip:] * factor).astype(BF16)
        pieces[w, 1] = dot(pmp_ref[w], g_ref[:part_rows, :])[skip:].astype(BF16)
    pieces[window] = jnp.zeros((2, tail, width), BF16)
    grad_copies = []
    for step in range(1, n):
        peer = lax.rem(me + step, n)
        chosen = jnp.int32(window)
        for w in range(window):
            chosen = jnp.where(order_ref[0, peer] == targets[w], w, chosen)
        staged[step] = pieces[chosen]
        copy = remote(staged.at[step], landed.at[step], grad_send, grad_recv, "ctx", me, n, step)
        copy.start()
        grad_copies.append(copy)

    for c in range(part_chunks):
        close_own(c, gains[c], deltas[c])
        both = atto_ref[:, cols(c)] * fades[c]
        for w in range(window):
            both = both + dot(vts[w], pp_ref[w, :, cols(c)])
        att_ref[cols(c), :] = jnp.transpose(both * inverses[c]).astype(BF16)
    att_out = pltpu.make_async_copy(att_ref, att_hbm, local_sem.at[6])
    att_out.start()
    own_k = dot(dso_ref[...], q_ref[...]) * factor
    own_v = dot(pmo_ref[...], g_ref[...])
    for copy in dcount_copies:
        copy.wait()
    counted = jnp.sum(
        jnp.sum(dcounts[...], axis=0).astype(F32), axis=1, keepdims=True
    )
    weight = weight_top / jnp.maximum(counted, 1.0)
    for c in range(chunks):
        back = dot(kt_own, dso_ref[:, cols(c)])
        if c < part_chunks:
            for w in range(window):
                back = back + dot(kts[w], dsp_ref[w, :, cols(c)])
        dq_ref[cols(c), :] = jnp.transpose(back * (weight * factor)).astype(BF16)
    dq_out = pltpu.make_async_copy(dq_ref, dq_hbm, local_sem.at[7])
    dq_out.start()

    for copy in grad_copies:
        copy.wait()
    arrived_k = landed[1, 0].astype(F32)
    arrived_v = landed[1, 1].astype(F32)
    for step in range(2, n):
        arrived_k = arrived_k + landed[step, 0].astype(F32)
        arrived_v = arrived_v + landed[step, 1].astype(F32)
    if skip:
        clear = jnp.zeros((skip, width), F32)
        arrived_k = jnp.concatenate([clear, arrived_k], axis=0)
        arrived_v = jnp.concatenate([clear, arrived_v], axis=0)
    heads_ref[my_head, 0] = ((own_k + arrived_k) * weight).astype(BF16)
    heads_ref[my_head, 1] = ((own_v + arrived_v) * weight).astype(BF16)
    head_copies = [
        remote(heads_ref.at[my_head], heads_ref.at[my_head], head_send, head_recv, "tensor", my_head, nt, step)
        for step in range(1, nt)
    ]
    for copy in head_copies:
        copy.start()
    for copy in head_copies:
        copy.wait()
    for i in range(2):
        mixed = None
        for h in range(nt):
            spread = jnp.where(pick == h, 1.0, 0.0).astype(BF16)
            term = dot_l(spread, heads_ref[h, i])
            mixed = term if mixed is None else mixed + term
        dkv_ref[i] = mixed.astype(BF16)
    dkv_out = pltpu.make_async_copy(dkv_ref, dkv_hbm, local_sem.at[8])
    dkv_out.start()
    att_out.wait()
    dq_out.wait()
    dkv_out.wait()


def local(query, key_value, grad_out, doc_lengths, stretch_order, loss_mask):
    _, rows, heads, width = query.shape
    n, nd, nt = lax.axis_size("ctx"), lax.axis_size("dp"), lax.axis_size("tensor")
    length = rows * n
    longest = length * 5 // 32
    window = (longest - 1 + rows - 1) // rows
    tail = rows if window > 1 else -(-(longest - 1) // 16) * 16
    reach = min(rows, longest - 1 + rows - rows * 1) if window == 1 else rows
    part_chunks = min(rows // CHUNK_TOKENS, -(-reach // CHUNK_TOKENS))
    docs = doc_lengths.shape[1]
    total = rows * heads
    part = part_chunks * CHUNK_TOKENS * heads
    chunk = CHUNK_TOKENS * heads
    chunks = rows // CHUNK_TOKENS
    weight_top = float(nd * query.shape[0] * length)
    sizes = (n, nd, nt, rows, heads, width, window, tail, docs, part_chunks, weight_top)
    dma = pltpu.SemaphoreType.DMA
    any_spec = pl.BlockSpec(memory_space=pl.ANY)
    att, dq, dkv = pl.pallas_call(
        functools.partial(kernel, sizes),
        out_shape=(
            jax.ShapeDtypeStruct((total, width), BF16),
            jax.ShapeDtypeStruct((total, width), BF16),
            jax.ShapeDtypeStruct((2, rows * nt, width), BF16),
        ),
        in_specs=[any_spec] * 6,
        out_specs=(any_spec,) * 3,
        scratch_shapes=[
            pltpu.VMEM((total, width), BF16),
            pltpu.VMEM((2, rows * nt, width), BF16),
            pltpu.VMEM((total, width), BF16),
            pltpu.SMEM((1, docs), jnp.int32),
            pltpu.SMEM((1, n), jnp.int32),
            pltpu.VMEM((1, rows), jnp.int32),
            pltpu.VMEM((total, width), BF16),
            pltpu.VMEM((total, width), BF16),
            pltpu.VMEM((2, rows * nt, width), BF16),
            pltpu.VMEM((n, 2, tail, width), BF16),
            pltpu.VMEM((n, 1, rows), jnp.int32),
            pltpu.VMEM((nd, 1, rows), jnp.int32),
            pltpu.VMEM((window + 1, 2, tail, width), BF16),
            pltpu.VMEM((n, 2, tail, width), BF16),
            pltpu.VMEM((n, 2, tail, width), BF16),
            pltpu.VMEM((nt, 2, rows, width), BF16),
            pltpu.VMEM((chunks, chunk, rows), BF16),
            pltpu.VMEM((rows, total), F32),
            pltpu.VMEM((rows, total), F32),
            pltpu.VMEM((width, part), F32),
            pltpu.VMEM((rows, total), BF16),
            pltpu.VMEM((rows, total), BF16),
            pltpu.VMEM((window, rows, part), BF16),
            pltpu.VMEM((window, rows, part), BF16),
            pltpu.VMEM((window, rows, part), BF16),
            dma((9,)),
            dma((n,)), dma((n,)),
            dma((n,)), dma((n,)),
            dma((nd,)), dma((nd,)),
            dma((n,)), dma((n,)),
            dma((nt,)), dma((nt,)),
        ],
        compiler_params=pltpu.CompilerParams(collective_id=0, has_side_effects=True),
        name="packed_attention",
    )(
        query.reshape(total, width),
        key_value.reshape(2, rows * nt, width),
        grad_out.reshape(total, width),
        doc_lengths,
        stretch_order,
        loss_mask,
    )
    return (
        att.reshape(query.shape),
        dq.reshape(query.shape),
        dkv.reshape(key_value.shape),
    )


def solution(mesh):
    placed = (
        P("dp", "ctx", "tensor", None),
        P(None, "dp", "ctx", None, None),
        P("dp", "ctx", "tensor", None),
        P("dp", None),
        P("dp", None),
        P("dp", "ctx"),
    )
    return jax.shard_map(
        local,
        mesh=mesh,
        in_specs=placed,
        out_specs=(
            P("dp", "ctx", "tensor", None),
            P("dp", "ctx", "tensor", None),
            P(None, "dp", "ctx", None, None),
        ),
        check_vma=False,
    )
```

time: 116 us -> 24.9 us (0.21)
  blocking collectives: 55 us -> 0 us
  Pallas kernels: 0 us -> 20.5 us
  waiting for transfers between devices: 16.4 us -> 0 us
  between operations: 15.5 us -> 0.65 us
  other arithmetic: 11.2 us -> 0 us
  loops' own time: 8.29 us -> 0 us
  matrix products: 5.35 us -> 0 us
    psum x1 -> x0, blocking collectives: 35.8 us -> none  [local(): counted = lax.psum(jnp.sum(loss_mask.astype(jnp.float32)), ('dp', 'ctx'))]
    pallas_call x0 -> x1, Pallas kernels: none -> 20.5 us  [local(): pl.pallas_call(functools.partial(kernel, sizes), out_shape=(jax.ShapeDtyp...]
    all_gather x2 -> x0, blocking collectives: 19.2 us -> none  [the longest x1 14 us: local(): fetched = lax.all_gather(own_pair, 'ctx', axis=1, tiled=True)]
    reduce_scatter x1 -> x0, waiting for transfers between devices: 16.3 us -> none  [local(): lax.psum_scatter(partial_value.astype(jnp.bfloat16), 'ctx', scatter_dimen...]
    another operation x6 -> x0, loops' own time: 8.29 us -> none  [the longest x1 2.77 us: local(): lax.fori_loop(0, slot_count, grad_step, (empty_rows, jnp.zeros((length, 2...]
    reduce_sum x13 -> x0, other arithmetic: 5.74 us -> none  [the longest x4 2.59 us: block_view(): holder = jnp.sum(jnp.where(order_row == target, stretch_ids, 0))]
    dot_general x14 -> x0, matrix products: 5.35 us -> none  [the longest x4 1.49 us: scores_of(): jnp.einsum('htd,kd->htk', queries, block_keys, preferred_element_type=jnp...]
    reduce_or x4 -> x0, other arithmetic: 3.01 us -> none  [the longest x2 1.54 us: forward_step(): jnp.any(visible)]
  transfers between devices with their start and end apart: 1 -> 0, of which waited for: 1 -> 0; matrix products, arithmetic and copies ran while one was open for 1% -> 0% of each run, Pallas kernels for 0% -> 0%
where the time goes in v1:
time: 24.9 us; the launch traced here: 24.8 us
  Pallas kernels  20.5 us (82%)
  local copies, waits for them, and re-layouts  3.61 us (14%)
  between operations  0.65 us (3%)
    pallas_call x1, Pallas kernels, local(): pl.pallas_call(functools.partial(kernel, sizes), out_shape=(jax.ShapeDtyp...  20.5 us
    unnamed x7, local copies, waits for them, and re-layouts  3.61 us

profile of v1, /device:TPU:0, one launch (start us, length us, event | category | flops | bytes accessed | tf_op | source)
XLA Modules:
  0.0 24.8 jit_solution(4022720053409538051)
XLA Ops:
  0.6 20.5 %packed_attention.1 = (bf16[2048,128]{1,0:T(8,128)(2,1)}, bf16[2048,128]{1,0:T(8,128)(2,1)}, bf16[2,256,128]{2,1,0:T(8,128)(2,1)}) custom-call(bf16[2048,128]{1,0:T(8,128)(2,1)} %bitcast.8, bf16[2,256,128]{2,1,0:T(8,128)(2,1)} %bitcast.12, bf16[2048,128]{1,0:T(8,128)(2,1)} %bitcast.9, s32[1,16]{1,0:T(1,128)} %doc_hbm.1, s32[1,4]{1,0:T(1,128)} %order_hbm.1, ...), custom_call_target="tpu_custom_call" | custom-call | tf_op jit(solution)/shard_map/packed_attention/pallas_call | solution.py:331
  21.1 0.0 copy-start
  21.2 1.9 %copy.13 = bf16[1,128,16,128]{3,2,1,0:T(8,128)(2,1)} copy(bf16[1,128,16,128]{3,2,1,0:T(8,128)(2,1)} %bitcast.11) | data formatting | bytes 1048576
  23.1 0.0 copy-done
  23.1 0.0 copy-start.1
  23.1 0.8 %copy.14 = bf16[1,128,16,128]{3,2,1,0:T(8,128)(2,1)} copy(bf16[1,128,16,128]{3,2,1,0:T(8,128)(2,1)S(1)} %bitcast.10) | data formatting | bytes 1048576
  23.9 0.2 copy-done.1
  24.1 0.7 %copy.15 = bf16[2,1,128,2,128]{4,3,2,1,0:T(2,128)(2,1)} copy(bf16[2,1,128,2,128]{4,3,2,1,0:T(2,128)(2,1)S(1)} %bitcast.13) | data formatting | bytes 262144
Async XLA Ops:
  21.1 1.9 %copy-start = (bf16[2048,128]{1,0:T(8,128)(2,1)S(1)}, bf16[2048,128]{1,0:T(8,128)(2,1)}, u32[]{:S(2)}) copy-start(bf16[2048,128]{1,0:T(8,128)(2,1)} %get-tuple-element.7) | copy-start | bytes 1572868
  23.1 1.0 %copy-start.1 = (bf16[2,256,128]{2,1,0:T(8,128)(2,1)S(1)}, bf16[2,256,128]{2,1,0:T(8,128)(2,1)}, u32[]{:S(2)}) copy-start(bf16[2,256,128]{2,1,0:T(8,128)(2,1)} %get-tuple-element.8) | copy-start | bytes 393220

commit v2 on v1

v2 whole, which is shorter than its diff:
```python
import functools
import math

import jax
import jax.numpy as jnp
from jax import lax
from jax.experimental import pallas as pl
from jax.experimental.pallas import tpu as pltpu
from jax.sharding import PartitionSpec as P

HIDDEN = -1e30
CHUNK_TOKENS = 16
KERNEL_VMEM = 32 * 1024 * 1024
F32 = jnp.float32
BF16 = jnp.bfloat16


def dot(left, right):
    return lax.dot_general(left, right, (((1,), (0,)), ((), ())), preferred_element_type=F32)


def dot_t(left, right):
    return lax.dot_general(left, right, (((1,), (1,)), ((), ())), preferred_element_type=F32)


def dot_l(left, right):
    return lax.dot_general(left, right, (((0,), (0,)), ((), ())), preferred_element_type=F32)


def kernel(
    sizes,
    q_hbm, kv_hbm, g_hbm, doc_hbm, order_hbm, mask_hbm,
    att_ref, dq_ref, dkv_ref,
    q_ref, kv_ref, g_ref, doc_ref, order_ref, mask_ref,
    k_all, v_all, counts, dcounts, pieces, staged, landed, owns, tails, base, spread,
    e_ref, po_ref, dpo_ref, atto_ref, pmo_ref, dso_ref, pf_ref, pmp_ref, dsp_ref,
    local_sem, kv_send, kv_recv, count_send, count_recv, dcount_send, dcount_recv,
    grad_send, grad_recv, own_send, own_recv, tail_send, tail_recv,
):
    n, nd, nt, rows, heads, width, window, tail, docs, part_chunks, weight_top = sizes
    me = lax.axis_index("ctx")
    my_dp = lax.axis_index("dp")
    my_head = lax.axis_index("tensor")
    chunk = CHUNK_TOKENS * heads
    chunks = rows // CHUNK_TOKENS
    part_rows = part_chunks * chunk
    skip = rows - tail
    factor = 1.0 / math.sqrt(width)
    steep = factor * math.log2(math.e)

    barrier = pltpu.get_barrier_semaphore()
    for axis, mine, count in (("ctx", me, n), ("dp", my_dp, nd), ("tensor", my_head, nt)):
        for step in range(1, count):
            pl.semaphore_signal(
                barrier,
                inc=1,
                device_id={axis: lax.rem(mine + step, count)},
                device_id_type=pl.DeviceIdType.MESH,
            )

    loads = [
        pltpu.make_async_copy(source, target, local_sem.at[i])
        for i, (source, target) in enumerate(
            (
                (kv_hbm, kv_ref),
                (mask_hbm, mask_ref),
                (doc_hbm, doc_ref),
                (order_hbm, order_ref),
                (q_hbm, q_ref),
                (g_hbm, g_ref),
            )
        )
    ]
    for load in loads:
        load.start()

    upper = (2 * me) // n
    short = me + upper * (n - 1 - 2 * me)
    spare = n - 1 - 2 * short
    side = 1 - 2 * upper
    far_first = []
    for k in range(n - 1):
        paired = k - spare
        distance = jnp.where(paired < 0, n - 1 - short - k, short - paired // 2)
        turn = jnp.where(paired < 0, 1, 1 - 2 * (paired % 2))
        far_first.append(me + side * turn * distance)

    def remote(source, target, send, recv, axis, peer):
        return pltpu.make_async_remote_copy(
            src_ref=source,
            dst_ref=target,
            send_sem=send,
            recv_sem=recv,
            device_id={axis: peer},
            device_id_type=pl.DeviceIdType.MESH,
        )

    gap = lax.broadcasted_iota(jnp.int32, (chunk, rows), 0) - heads * lax.broadcasted_iota(
        jnp.int32, (chunk, rows), 1
    )
    for c in range(chunks):
        moved = gap + c * chunk
        e_ref[c] = jnp.where((moved >= 0) & (moved < heads), 1.0, 0.0).astype(BF16)
    pick = (
        lax.broadcasted_iota(jnp.int32, (rows, rows * nt), 1)
        - nt * lax.broadcasted_iota(jnp.int32, (rows, rows * nt), 0)
    )
    own_pick = jnp.where(pick == my_head, 1.0, 0.0).astype(BF16)

    loads[0].wait()
    k_own = dot(own_pick, kv_ref[0]).astype(BF16)
    k_all[me] = k_own[skip:]
    v_own = dot(own_pick, kv_ref[1]).astype(BF16)
    v_all[me] = v_own[skip:]
    loads[1].wait()
    counts[me] = mask_ref[...]
    pl.semaphore_wait(barrier, n + nd + nt - 3)

    def kv_copy(i, source, peer):
        held = (k_all, v_all)[i]
        return remote(
            held.at[me], held.at[source], kv_send.at[i, peer], kv_recv.at[i, source], "ctx", peer
        )

    def count_copy(source, peer):
        return remote(
            counts.at[me], counts.at[source], count_send.at[peer], count_recv.at[source], "ctx", peer
        )

    for peer in far_first:
        kv_copy(0, me, peer).start()
    for peer in far_first:
        kv_copy(1, me, peer).start()
    for peer in far_first:
        count_copy(me, peer).start()

    loads[2].wait()
    loads[3].wait()
    own = order_ref[0, me]
    token_row = lax.broadcasted_iota(jnp.int32, (1, rows), 1)
    place_row = own * rows + token_row
    start_row = jnp.zeros((1, rows), jnp.int32)
    bound = jnp.int32(0)
    for j in range(docs):
        bound = bound + doc_ref[0, j]
        start_row = jnp.where(bound <= place_row, bound, start_row)
    key_rows = lax.broadcasted_iota(jnp.int32, (rows, rows), 0)

    def bias_of(target):
        key_places = target * rows + key_rows
        seen = (key_places >= start_row) & (key_places <= place_row)
        return jnp.where(seen, 0.0, HIDDEN).astype(BF16)

    def flipped(block):
        return jnp.transpose(block.astype(F32)).astype(BF16)

    wide_own = jnp.concatenate([k_own, bias_of(own)], axis=1)
    kt_own = flipped(k_own)
    vt_own = flipped(v_own)
    mask_rows = jnp.broadcast_to(mask_ref[...].astype(F32), (8, rows)).astype(BF16)
    turned = lax.broadcasted_iota(jnp.int32, (rows * nt, rows), 0) - nt * lax.broadcasted_iota(
        jnp.int32, (rows * nt, rows), 1
    )
    for h in range(nt):
        spread[h] = jnp.where(turned == h, 1.0, 0.0).astype(BF16)

    def cols(c):
        return pl.ds(c * chunk, chunk)

    def wide_queries(c):
        return jnp.concatenate([q_ref[cols(c), :], e_ref[c]], axis=1)

    loads[4].wait()
    loads[5].wait()
    top, total, drift, kept = [], [], [], []

    def close_own(c, gain, delta):
        masked = po_ref[:, cols(c)] * gain
        pmo_ref[:, cols(c)] = masked.astype(BF16)
        dso_ref[:, cols(c)] = (masked * (dpo_ref[:, cols(c)] - delta)).astype(BF16)

    for c in range(chunks):
        scores = dot_t(wide_own, wide_queries(c))
        grads = dot_t(v_own, g_ref[cols(c), :])
        highest = jnp.max(scores, axis=0, keepdims=True)
        raised = jnp.exp2((scores - highest) * steep)
        summed = jnp.sum(raised, axis=0, keepdims=True)
        drifted = jnp.sum(raised * grads, axis=0, keepdims=True)
        top.append(highest)
        total.append(summed)
        drift.append(drifted)
        kept.append(dot_t(mask_rows, e_ref[c])[0:1])
        po_ref[:, cols(c)] = raised
        dpo_ref[:, cols(c)] = grads
        own_part = dot(vt_own, raised.astype(BF16))
        if c < part_chunks:
            atto_ref[:, cols(c)] = own_part
        else:
            inverse = 1.0 / summed
            close_own(c, kept[c] * inverse, drifted * inverse)
            att_ref[cols(c), :] = jnp.transpose(own_part * inverse).astype(BF16)

    def others():
        return [lax.rem(me + step, n) for step in range(1, n)]

    def filled(block):
        if not skip:
            return block
        return jnp.concatenate([jnp.zeros((skip, width), block.dtype), block], axis=0)

    def grad_copy(i, step):
        return remote(
            staged.at[i, step],
            landed.at[i, step],
            grad_send.at[i, step],
            grad_recv.at[i, step],
            "ctx",
            lax.rem(me + step, n),
        )

    def scatter(i):
        pieces[i, window] = jnp.zeros((tail, width), BF16)
        for step in range(1, n):
            peer = lax.rem(me + step, n)
            chosen = jnp.int32(window)
            for w in range(window):
                chosen = jnp.where(order_ref[0, peer] == targets[w], w, chosen)
            staged[i, step] = pieces[i, chosen]
        for peer in far_first:
            grad_copy(i, lax.rem(peer - me + n, n)).start()

    for peer in others():
        kv_copy(0, peer, peer).wait()
    targets = [own - 1 - w for w in range(window)]
    holders = []
    for w in range(window):
        holder = jnp.int32(0)
        for j in range(n):
            holder = holder + jnp.where(order_ref[0, j] == targets[w], j, 0)
        holders.append(holder)
    keys = [filled(k_all[holders[w]]) for w in range(window)]
    wide = [jnp.concatenate([keys[w], bias_of(targets[w])], axis=1) for w in range(window)]
    gains, inverses, fades = [], [], []
    for c in range(part_chunks):
        queries = wide_queries(c)
        scores = [dot_t(wide[w], queries) for w in range(window)]
        highest = top[c]
        for w in range(window):
            highest = jnp.maximum(highest, jnp.max(scores[w], axis=0, keepdims=True))
        fade = jnp.exp2((top[c] - highest) * steep)
        summed = total[c] * fade
        raised = []
        for w in range(window):
            part = jnp.exp2((scores[w] - highest) * steep)
            summed = summed + jnp.sum(part, axis=0, keepdims=True)
            pf_ref[w, :, cols(c)] = part
            raised.append(part)
        inverse = 1.0 / summed
        gain = kept[c] * inverse
        for w in range(window):
            pmp_ref[w, :, cols(c)] = (raised[w] * gain).astype(BF16)
        gains.append(gain)
        inverses.append(inverse)
        fades.append(fade)
    for w in range(window):
        pieces[1, w] = dot(pmp_ref[w], g_ref[:part_rows, :])[skip:].astype(BF16)
    scatter(1)

    for peer in others():
        kv_copy(1, peer, peer).wait()
    values = [filled(v_all[holders[w]]) for w in range(window)]
    deltas = []
    for c in range(part_chunks):
        grads = [dot_t(values[w], g_ref[cols(c), :]) for w in range(window)]
        raised = [pf_ref[w, :, cols(c)] for w in range(window)]
        drifted = drift[c] * fades[c]
        for w in range(window):
            drifted = drifted + jnp.sum(raised[w] * grads[w], axis=0, keepdims=True)
        delta = drifted * inverses[c]
        for w in range(window):
            dsp_ref[w, :, cols(c)] = (raised[w] * gains[c] * (grads[w] - delta)).astype(BF16)
        deltas.append(delta)
    for w in range(window):
        pieces[0, w] = (dot(dsp_ref[w], q_ref[:part_rows, :])[skip:] * factor).astype(BF16)
    scatter(0)

    for peer in others():
        count_copy(peer, peer).wait()
    dcounts[my_dp] = jnp.sum(counts[...], axis=0)
    dcount_copies = [
        remote(
            dcounts.at[my_dp],
            dcounts.at[my_dp],
            dcount_send.at[step],
            dcount_recv.at[step],
            "dp",
            lax.rem(my_dp + step, nd),
        )
        for step in range(1, nd)
    ]
    for copy in dcount_copies:
        copy.start()

    def head_copies(buffer, send, recv):
        return [
            remote(
                buffer.at[my_head],
                buffer.at[my_head],
                send.at[step],
                recv.at[step],
                "tensor",
                lax.rem(my_head + step, nt),
            )
            for step in range(1, nt)
        ]

    for c in range(part_chunks):
        close_own(c, gains[c] * fades[c], deltas[c])
    owns[my_head, 0] = (dot(dso_ref[...], q_ref[...]) * factor).astype(BF16)
    owns[my_head, 1] = dot(pmo_ref[...], g_ref[...]).astype(BF16)
    own_copies = head_copies(owns, own_send, own_recv)
    for copy in own_copies:
        copy.start()

    vts = [flipped(values[w]) for w in range(window)]
    for c in range(part_chunks):
        both = atto_ref[:, cols(c)] * fades[c]
        for w in range(window):
            both = both + dot(vts[w], pf_ref[w, :, cols(c)].astype(BF16))
        att_ref[cols(c), :] = jnp.transpose(both * inverses[c]).astype(BF16)

    def forward(i):
        for step in range(1, n):
            grad_copy(i, step).wait()
        arrived = landed[i, 1].astype(F32)
        for step in range(2, n):
            arrived = arrived + landed[i, step].astype(F32)
        tails[i, my_head] = arrived.astype(BF16)
        copies = head_copies(tails.at[i], tail_send.at[i], tail_recv.at[i])
        for copy in copies:
            copy.start()
        return copies

    tail_v = forward(1)
    for copy in dcount_copies:
        copy.wait()
    counted = jnp.sum(
        jnp.sum(dcounts[...], axis=0).astype(F32), axis=1, keepdims=True
    )
    weight = weight_top / jnp.maximum(counted, 1.0)
    kts = [flipped(keys[w]) for w in range(window)]
    for c in range(chunks):
        back = dot(kt_own, dso_ref[:, cols(c)])
        if c < part_chunks:
            for w in range(window):
                back = back + dot(kts[w], dsp_ref[w, :, cols(c)])
        dq_ref[cols(c), :] = jnp.transpose(back * (weight * factor)).astype(BF16)

    def mixed(blocks):
        result = dot(spread[0], blocks[0])
        for h in range(1, nt):
            result = result + dot(spread[h], blocks[h])
        return result

    for copy in own_copies:
        copy.wait()
    for i in range(2):
        base[i] = mixed([owns[h, i] for h in range(nt)])

    def finish(i, copies):
        for copy in copies:
            copy.wait()
        arrived = mixed([filled(tails[i, h]) for h in range(nt)])
        dkv_ref[i] = ((base[i] + arrived) * weight).astype(BF16)

    tail_k = forward(0)
    finish(1, tail_v)
    finish(0, tail_k)


def write_out(att_ref, dq_ref, dkv_ref, att_hbm, dq_hbm, dkv_hbm, sems):
    copies = [
        pltpu.make_async_copy(source, target, sems.at[i])
        for i, (source, target) in enumerate(
            ((dkv_ref, dkv_hbm), (att_ref, att_hbm), (dq_ref, dq_hbm))
        )
    ]
    for copy in copies:
        copy.start()
    for copy in copies:
        copy.wait()


def local(query, key_value, grad_out, doc_lengths, stretch_order, loss_mask):
    _, rows, heads, width = query.shape
    n, nd, nt = lax.axis_size("ctx"), lax.axis_size("dp"), lax.axis_size("tensor")
    length = rows * n
    longest = length * 5 // 32
    window = (longest - 1 + rows - 1) // rows
    tail = rows if window > 1 else -(-(longest - 1) // 16) * 16
    reach = min(rows, longest - 1) if window == 1 else rows
    part_chunks = min(rows // CHUNK_TOKENS, -(-reach // CHUNK_TOKENS))
    docs = doc_lengths.shape[1]
    total = rows * heads
    part = part_chunks * CHUNK_TOKENS * heads
    chunk = CHUNK_TOKENS * heads
    chunks = rows // CHUNK_TOKENS
    weight_top = float(nd * query.shape[0] * length)
    sizes = (n, nd, nt, rows, heads, width, window, tail, docs, part_chunks, weight_top)
    dma = pltpu.SemaphoreType.DMA
    any_spec = pl.BlockSpec(memory_space=pl.ANY)
    vmem_spec = pl.BlockSpec(memory_space=pltpu.VMEM)
    shapes = (
        jax.ShapeDtypeStruct((total, width), BF16),
        jax.ShapeDtypeStruct((total, width), BF16),
        jax.ShapeDtypeStruct((2, rows * nt, width), BF16),
    )
    results = pl.pallas_call(
        functools.partial(kernel, sizes),
        out_shape=shapes,
        in_specs=[pl.BlockSpec(memory_space=pltpu.MemorySpace.HBM)] * 6,
        out_specs=(vmem_spec,) * 3,
        scratch_shapes=[
            pltpu.VMEM((total, width), BF16),
            pltpu.VMEM((2, rows * nt, width), BF16),
            pltpu.VMEM((total, width), BF16),
            pltpu.SMEM((1, docs), jnp.int32),
            pltpu.SMEM((1, n), jnp.int32),
            pltpu.VMEM((1, rows), jnp.int32),
            pltpu.VMEM((n, tail, width), BF16),
            pltpu.VMEM((n, tail, width), BF16),
            pltpu.VMEM((n, 1, rows), jnp.int32),
            pltpu.VMEM((nd, 1, rows), jnp.int32),
            pltpu.VMEM((2, window + 1, tail, width), BF16),
            pltpu.VMEM((2, n, tail, width), BF16),
            pltpu.VMEM((2, n, tail, width), BF16),
            pltpu.VMEM((nt, 2, rows, width), BF16),
            pltpu.VMEM((2, nt, tail, width), BF16),
            pltpu.VMEM((2, rows * nt, width), F32),
            pltpu.VMEM((nt, rows * nt, rows), BF16),
            pltpu.VMEM((chunks, chunk, rows), BF16),
            pltpu.VMEM((rows, total), F32),
            pltpu.VMEM((rows, total), F32),
            pltpu.VMEM((width, part), F32),
            pltpu.VMEM((rows, total), BF16),
            pltpu.VMEM((rows, total), BF16),
            pltpu.VMEM((window, rows, part), F32),
            pltpu.VMEM((window, rows, part), BF16),
            pltpu.VMEM((window, rows, part), BF16),
            dma((6,)),
            dma((2, n)), dma((2, n)),
            dma((n,)), dma((n,)),
            dma((nd,)), dma((nd,)),
            dma((2, n)), dma((2, n)),
            dma((nt,)), dma((nt,)),
            dma((2, nt)), dma((2, nt)),
        ],
        compiler_params=pltpu.CompilerParams(
            collective_id=0, has_side_effects=True, vmem_limit_bytes=KERNEL_VMEM
        ),
        name="packed_attention",
    )(
        *(
            pltpu.with_memory_space_constraint(array, pltpu.MemorySpace.HBM)
            for array in (
                query.reshape(total, width),
                key_value.reshape(2, rows * nt, width),
                grad_out.reshape(total, width),
                doc_lengths,
                stretch_order,
                loss_mask,
            )
        )
    )
    att, dq, dkv = pl.pallas_call(
        write_out,
        out_shape=shapes,
        in_specs=[vmem_spec] * 3,
        out_specs=(any_spec,) * 3,
        scratch_shapes=[dma((3,))],
        compiler_params=pltpu.CompilerParams(vmem_limit_bytes=KERNEL_VMEM),
        name="write_out",
    )(*results)
    return (
        att.reshape(query.shape),
        dq.reshape(query.shape),
        dkv.reshape(key_value.shape),
    )


def solution(mesh):
    placed = (
        P("dp", "ctx", "tensor", None),
        P(None, "dp", "ctx", None, None),
        P("dp", "ctx", "tensor", None),
        P("dp", None),
        P("dp", None),
        P("dp", "ctx"),
    )
    return jax.shard_map(
        local,
        mesh=mesh,
        in_specs=placed,
        out_specs=(
            P("dp", "ctx", "tensor", None),
            P("dp", "ctx", "tensor", None),
            P(None, "dp", "ctx", None, None),
        ),
        check_vma=False,
    )
```

time: 24.9 us -> 19.9 us (0.80)
  local copies, waits for them, and re-layouts: 3.61 us -> 0 us
  Pallas kernels: 20.5 us -> 19.2 us
    unnamed x7 -> x0, local copies, waits for them, and re-layouts: 3.61 us -> none
    pallas_call x1 -> x2, Pallas kernels: 20.5 us -> 19.2 us  [the longest x1 18.1 us: local(): pl.pallas_call(functools.partial(kernel, sizes), out_shape=shapes, in_spe...]
where the time goes in v2:
time: 19.9 us; the launch traced here: 19.8 us
  Pallas kernels  19.2 us (96%)
  between operations  0.64 us (3%)
    pallas_call x1, Pallas kernels, local(): pl.pallas_call(functools.partial(kernel, sizes), out_shape=shapes, in_spe...  18.1 us
    pallas_call x1, Pallas kernels, local(): pl.pallas_call(write_out, out_shape=shapes, in_specs=[vmem_spec] * 3, out...  1.04 us

profile of v2, /device:TPU:0, one launch (start us, length us, event | category | flops | bytes accessed | tf_op | source)
XLA Modules:
  0.0 19.8 jit_solution(579958241563155403)
XLA Ops:
  0.6 18.1 %packed_attention.1 = (bf16[2048,128]{1,0:T(8,128)(2,1)S(1)}, bf16[2048,128]{1,0:T(8,128)(2,1)S(1)}, bf16[2,256,128]{2,1,0:T(8,128)(2,1)S(1)}) custom-call(bf16[2048,128]{1,0:T(8,128)(2,1)} %bitcast.8, bf16[2,256,128]{2,1,0:T(8,128)(2,1)} %bitcast.10, bf16[2048,128]{1,0:T(8,128)(2,1)} %bitcast.9, s32[1,16]{1,0:T(1,128)} %doc_hbm.1, s32[1,4]{1,0:T(1,128)} %order_hbm.1, ...), custom_call_target="tpu_custom_call" | custom-call | tf_op jit(solution)/shard_map/packed_attention/pallas_call | solution.py:418
  18.8 1.0 %write_out.1 = (bf16[2048,128]{1,0:T(8,128)(2,1)}, bf16[2048,128]{1,0:T(8,128)(2,1)}, bf16[2,256,128]{2,1,0:T(8,128)(2,1)}) custom-call(bf16[2048,128]{1,0:T(8,128)(2,1)S(1)} %get-tuple-element.9.att_ref, bf16[2048,128]{1,0:T(8,128)(2,1)S(1)} %get-tuple-element.10.dq_ref, bf16[2,256,128]{2,1,0:T(8,128)(2,1)S(1)} %get-tuple-element.11.dkv_ref), custom_call_target="tpu_custom_call" | custom-call | tf_op jit(solution)/shard_map/write_out/pallas_call | solution.py:475

commit v3 on v2

--- a/solution.py
+++ b/solution.py
@@ -11,6 +11,7 @@
 HIDDEN = -1e30
 CHUNK_TOKENS = 16
 KERNEL_VMEM = 32 * 1024 * 1024
+OUT_PIECES = 4
 F32 = jnp.float32
 BF16 = jnp.bfloat16
 
@@ -37,7 +38,7 @@
     local_sem, kv_send, kv_recv, count_send, count_recv, dcount_send, dcount_recv,
     grad_send, grad_recv, own_send, own_recv, tail_send, tail_recv,
 ):
-    n, nd, nt, rows, heads, width, window, tail, docs, part_chunks, weight_top = sizes
+    n, nd, nt, rows, heads, width, window, tail, docs, longest, part_chunks, weight_top = sizes
     me = lax.axis_index("ctx")
     my_dp = lax.axis_index("dp")
     my_head = lax.axis_index("tensor")
@@ -174,14 +175,30 @@
     loads[5].wait()
     top, total, drift, kept = [], [], [], []
 
+    def seen_rows(c, behind):
+        first = c * CHUNK_TOKENS + behind * rows - (longest - 1)
+        low = max(0, first // 16 * 16)
+        return low, rows if behind else (c + 1) * CHUNK_TOKENS
+
+    def padded(block, low, high):
+        block = block.astype(BF16)
+        parts = [block]
+        if low:
+            parts.insert(0, jnp.zeros((low, chunk), BF16))
+        if high < rows:
+            parts.append(jnp.zeros((rows - high, chunk), BF16))
+        return jnp.concatenate(parts, axis=0) if len(parts) > 1 else block
+
     def close_own(c, gain, delta):
-        masked = po_ref[:, cols(c)] * gain
-        pmo_ref[:, cols(c)] = masked.astype(BF16)
-        dso_ref[:, cols(c)] = (masked * (dpo_ref[:, cols(c)] - delta)).astype(BF16)
+        low, high = seen_rows(c, 0)
+        masked = po_ref[low:high, cols(c)] * gain
+        pmo_ref[:, cols(c)] = padded(masked, low, high)
+        dso_ref[:, cols(c)] = padded(masked * (dpo_ref[low:high, cols(c)] - delta), low, high)
 
     for c in range(chunks):
-        scores = dot_t(wide_own, wide_queries(c))
-        grads = dot_t(v_own, g_ref[cols(c), :])
+        low, high = seen_rows(c, 0)
+        scores = dot_t(wide_own[low:high], wide_queries(c))
+        grads = dot_t(v_own[low:high], g_ref[cols(c), :])
         highest = jnp.max(scores, axis=0, keepdims=True)
         raised = jnp.exp2((scores - highest) * steep)
         summed = jnp.sum(raised, axis=0, keepdims=True)
@@ -190,9 +207,9 @@
         total.append(summed)
         drift.append(drifted)
         kept.append(dot_t(mask_rows, e_ref[c])[0:1])
-        po_ref[:, cols(c)] = raised
-        dpo_ref[:, cols(c)] = grads
-        own_part = dot(vt_own, raised.astype(BF16))
+        po_ref[low:high, cols(c)] = raised
+        dpo_ref[low:high, cols(c)] = grads
+        own_part = dot(vt_own, padded(raised, low, high))
         if c < part_chunks:
             atto_ref[:, cols(c)] = own_part
         else:
@@ -243,7 +260,8 @@
     gains, inverses, fades = [], [], []
     for c in range(part_chunks):
         queries = wide_queries(c)
-        scores = [dot_t(wide[w], queries) for w in range(window)]
+        low = [seen_rows(c, w + 1)[0] for w in range(window)]
+        scores = [dot_t(wide[w][low[w]:], queries) for w in range(window)]
         highest = top[c]
         for w in range(window):
             highest = jnp.maximum(highest, jnp.max(scores[w], axis=0, keepdims=True))
@@ -253,12 +271,12 @@
         for w in range(window):
             part = jnp.exp2((scores[w] - highest) * steep)
             summed = summed + jnp.sum(part, axis=0, keepdims=True)
-            pf_ref[w, :, cols(c)] = part
+            pf_ref[w, low[w]:, cols(c)] = part
             raised.append(part)
         inverse = 1.0 / summed
         gain = kept[c] * inverse
         for w in range(window):
-            pmp_ref[w, :, cols(c)] = (raised[w] * gain).astype(BF16)
+            pmp_ref[w, :, cols(c)] = padded(raised[w] * gain, low[w], rows)
         gains.append(gain)
         inverses.append(inverse)
         fades.append(fade)
@@ -271,14 +289,17 @@
     values = [filled(v_all[holders[w]]) for w in range(window)]
     deltas = []
     for c in range(part_chunks):
-        grads = [dot_t(values[w], g_ref[cols(c), :]) for w in range(window)]
-        raised = [pf_ref[w, :, cols(c)] for w in range(window)]
+        low = [seen_rows(c, w + 1)[0] for w in range(window)]
+        grads = [dot_t(values[w][low[w]:], g_ref[cols(c), :]) for w in range(window)]
+        raised = [pf_ref[w, low[w]:, cols(c)] for w in range(window)]
         drifted = drift[c] * fades[c]
         for w in range(window):
             drifted = drifted + jnp.sum(raised[w] * grads[w], axis=0, keepdims=True)
         delta = drifted * inverses[c]
         for w in range(window):
-            dsp_ref[w, :, cols(c)] = (raised[w] * gains[c] * (grads[w] - delta)).astype(BF16)
+            dsp_ref[w, :, cols(c)] = padded(
+                raised[w] * gains[c] * (grads[w] - delta), low[w], rows
+            )
         deltas.append(delta)
     for w in range(window):
         pieces[0, w] = (dot(dsp_ref[w], q_ref[:part_rows, :])[skip:] * factor).astype(BF16)
@@ -326,7 +347,8 @@
     for c in range(part_chunks):
         both = atto_ref[:, cols(c)] * fades[c]
         for w in range(window):
-            both = both + dot(vts[w], pf_ref[w, :, cols(c)].astype(BF16))
+            low = seen_rows(c, w + 1)[0]
+            both = both + dot(vts[w], padded(pf_ref[w, low:, cols(c)], low, rows))
         att_ref[cols(c), :] = jnp.transpose(both * inverses[c]).astype(BF16)
 
     def forward(i):
@@ -379,11 +401,15 @@
 
 
 def write_out(att_ref, dq_ref, dkv_ref, att_hbm, dq_hbm, dkv_hbm, sems):
+    pairs = [(dkv_ref.at[i], dkv_hbm.at[i]) for i in range(dkv_ref.shape[0])]
+    piece = att_ref.shape[0] // OUT_PIECES
+    for i in range(OUT_PIECES):
+        span = pl.ds(i * piece, piece)
+        pairs.append((att_ref.at[span], att_hbm.at[span]))
+        pairs.append((dq_ref.at[span], dq_hbm.at[span]))
     copies = [
         pltpu.make_async_copy(source, target, sems.at[i])
-        for i, (source, target) in enumerate(
-            ((dkv_ref, dkv_hbm), (att_ref, att_hbm), (dq_ref, dq_hbm))
-        )
+        for i, (source, target) in enumerate(pairs)
     ]
     for copy in copies:
         copy.start()
@@ -406,7 +432,7 @@
     chunk = CHUNK_TOKENS * heads
     chunks = rows // CHUNK_TOKENS
     weight_top = float(nd * query.shape[0] * length)
-    sizes = (n, nd, nt, rows, heads, width, window, tail, docs, part_chunks, weight_top)
+    sizes = (n, nd, nt, rows, heads, width, window, tail, docs, longest, part_chunks, weight_top)
     dma = pltpu.SemaphoreType.DMA
     any_spec = pl.BlockSpec(memory_space=pl.ANY)
     vmem_spec = pl.BlockSpec(memory_space=pltpu.VMEM)
@@ -477,7 +503,7 @@
         out_shape=shapes,
         in_specs=[vmem_spec] * 3,
         out_specs=(any_spec,) * 3,
-        scratch_shapes=[dma((3,))],
+        scratch_shapes=[dma((2 + 2 * OUT_PIECES,))],
         compiler_params=pltpu.CompilerParams(vmem_limit_bytes=KERNEL_VMEM),
         name="write_out",
     )(*results)

time: 19.9 us -> 19.8 us (level)
  Pallas kernels: 19.2 us -> 19 us
    pallas_call x1, Pallas kernels: 18.1 us -> 17.9 us  [local(): pl.pallas_call(functools.partial(kernel, sizes), out_shape=shapes, in_spe...]
where the time goes in v3:
time: 19.8 us; the launch traced here: 19.6 us
  Pallas kernels  19 us (96%)
  between operations  0.64 us (3%)
    pallas_call x1, Pallas kernels, local(): pl.pallas_call(functools.partial(kernel, sizes), out_shape=shapes, in_spe...  17.9 us
    pallas_call x1, Pallas kernels, local(): pl.pallas_call(write_out, out_shape=shapes, in_specs=[vmem_spec] * 3, out...  1.09 us

profile of v3, /device:TPU:0, one launch (start us, length us, event | category | flops | bytes accessed | tf_op | source)
XLA Modules:
  0.0 19.6 jit_solution(87299329873029711)
XLA Ops:
  0.6 17.9 %packed_attention.1 = (bf16[2048,128]{1,0:T(8,128)(2,1)S(1)}, bf16[2048,128]{1,0:T(8,128)(2,1)S(1)}, bf16[2,256,128]{2,1,0:T(8,128)(2,1)S(1)}) custom-call(bf16[2048,128]{1,0:T(8,128)(2,1)} %bitcast.8, bf16[2,256,128]{2,1,0:T(8,128)(2,1)} %bitcast.10, bf16[2048,128]{1,0:T(8,128)(2,1)} %bitcast.9, s32[1,16]{1,0:T(1,128)} %doc_hbm.1, s32[1,4]{1,0:T(1,128)} %order_hbm.1, ...), custom_call_target="tpu_custom_call" | custom-call | tf_op jit(solution)/shard_map/packed_attention/pallas_call | solution.py:444
  18.5 1.1 %write_out.1 = (bf16[2048,128]{1,0:T(8,128)(2,1)}, bf16[2048,128]{1,0:T(8,128)(2,1)}, bf16[2,256,128]{2,1,0:T(8,128)(2,1)}) custom-call(bf16[2048,128]{1,0:T(8,128)(2,1)S(1)} %get-tuple-element.9.att_ref, bf16[2048,128]{1,0:T(8,128)(2,1)S(1)} %get-tuple-element.10.dq_ref, bf16[2,256,128]{2,1,0:T(8,128)(2,1)S(1)} %get-tuple-element.11.dkv_ref), custom_call_target="tpu_custom_call" | custom-call | tf_op jit(solution)/shard_map/write_out/pallas_call | solution.py:501

commit v4 on v3

--- a/solution.py
+++ b/solution.py
@@ -35,7 +35,7 @@
     q_ref, kv_ref, g_ref, doc_ref, order_ref, mask_ref,
     k_all, v_all, counts, dcounts, pieces, staged, landed, owns, tails, base, spread,
     e_ref, po_ref, dpo_ref, atto_ref, pmo_ref, dso_ref, pf_ref, pmp_ref, dsp_ref,
-    local_sem, kv_send, kv_recv, count_send, count_recv, dcount_send, dcount_recv,
+    local_sem, answers, kv_send, kv_recv, count_send, count_recv, dcount_send, dcount_recv,
     grad_send, grad_recv, own_send, own_recv, tail_send, tail_recv,
 ):
     n, nd, nt, rows, heads, width, window, tail, docs, longest, part_chunks, weight_top = sizes
@@ -50,12 +50,23 @@
     steep = factor * math.log2(math.e)
 
     barrier = pltpu.get_barrier_semaphore()
-    for axis, mine, count in (("ctx", me, n), ("dp", my_dp, nd), ("tensor", my_head, nt)):
+    for axis, mine, count in (("ctx", me, n), ("tensor", my_head, nt)):
         for step in range(1, count):
             pl.semaphore_signal(
                 barrier,
                 inc=1,
                 device_id={axis: lax.rem(mine + step, count)},
+                device_id_type=pl.DeviceIdType.MESH,
+            )
+
+    for step in range(1, nd):
+
+        @pl.when(my_dp + step < nd)
+        def _greet():
+            pl.semaphore_signal(
+                barrier,
+                inc=1,
+                device_id={"dp": lax.rem(my_dp + step, nd)},
                 device_id_type=pl.DeviceIdType.MESH,
             )
 
@@ -115,7 +126,7 @@
     v_all[me] = v_own[skip:]
     loads[1].wait()
     counts[me] = mask_ref[...]
-    pl.semaphore_wait(barrier, n + nd + nt - 3)
+    pl.semaphore_wait(barrier, n + nt - 2 + my_dp)
 
     def kv_copy(i, source, peer):
         held = (k_all, v_all)[i]
@@ -131,9 +142,19 @@
     for peer in far_first:
         kv_copy(0, me, peer).start()
     for peer in far_first:
+        count_copy(me, peer).start()
+    for peer in far_first:
         kv_copy(1, me, peer).start()
-    for peer in far_first:
-        count_copy(me, peer).start()
+    for step in range(1, nd):
+
+        @pl.when(my_dp >= step)
+        def _answer():
+            pl.semaphore_signal(
+                answers,
+                inc=1,
+                device_id={"dp": lax.rem(my_dp - step + nd, nd)},
+                device_id_type=pl.DeviceIdType.MESH,
+            )
 
     loads[2].wait()
     loads[3].wait()
@@ -285,6 +306,28 @@
     scatter(1)
 
     for peer in others():
+        count_copy(peer, peer).wait()
+    dcounts[my_dp] = jnp.sum(counts[...], axis=0)
+    dcount_copies = [
+        remote(
+            dcounts.at[my_dp],
+            dcounts.at[my_dp],
+            dcount_send.at[step],
+            dcount_recv.at[step],
+            "dp",
+            lax.rem(my_dp + step, nd),
+        )
+        for step in range(1, nd)
+    ]
+
+    @pl.when(my_dp < nd - 1)
+    def _answered():
+        pl.semaphore_wait(answers, nd - 1 - my_dp)
+
+    for copy in dcount_copies:
+        copy.start()
+
+    for peer in others():
         kv_copy(1, peer, peer).wait()
     values = [filled(v_all[holders[w]]) for w in range(window)]
     deltas = []
@@ -305,23 +348,6 @@
         pieces[0, w] = (dot(dsp_ref[w], q_ref[:part_rows, :])[skip:] * factor).astype(BF16)
     scatter(0)
 
-    for peer in others():
-        count_copy(peer, peer).wait()
-    dcounts[my_dp] = jnp.sum(counts[...], axis=0)
-    dcount_copies = [
-        remote(
-            dcounts.at[my_dp],
-            dcounts.at[my_dp],
-            dcount_send.at[step],
-            dcount_recv.at[step],
-            "dp",
-            lax.rem(my_dp + step, nd),
-        )
-        for step in range(1, nd)
-    ]
-    for copy in dcount_copies:
-        copy.start()
-
     def head_copies(buffer, send, recv):
         return [
             remote(
@@ -364,6 +390,24 @@
         return copies
 
     tail_v = forward(1)
+    def mixed(blocks):
+        result = dot(spread[0], blocks[0])
+        for h in range(1, nt):
+            result = result + dot(spread[h], blocks[h])
+        return result
+
+    for copy in own_copies:
+        copy.wait()
+    for i in range(2):
+        base[i] = mixed([owns[h, i] for h in range(nt)])
+
+    def finish(i, copies):
+        for copy in copies:
+            copy.wait()
+        arrived = mixed([filled(tails[i, h]) for h in range(nt)])
+        dkv_ref[i] = ((base[i] + arrived) * weight).astype(BF16)
+
+    tail_k = forward(0)
     for copy in dcount_copies:
         copy.wait()
     counted = jnp.sum(
@@ -378,24 +422,6 @@
                 back = back + dot(kts[w], dsp_ref[w, :, cols(c)])
         dq_ref[cols(c), :] = jnp.transpose(back * (weight * factor)).astype(BF16)
 
-    def mixed(blocks):
-        result = dot(spread[0], blocks[0])
-        for h in range(1, nt):
-            result = result + dot(spread[h], blocks[h])
-        return result
-
-    for copy in own_copies:
-        copy.wait()
-    for i in range(2):
-        base[i] = mixed([owns[h, i] for h in range(nt)])
-
-    def finish(i, copies):
-        for copy in copies:
-            copy.wait()
-        arrived = mixed([filled(tails[i, h]) for h in range(nt)])
-        dkv_ref[i] = ((base[i] + arrived) * weight).astype(BF16)
-
-    tail_k = forward(0)
     finish(1, tail_v)
     finish(0, tail_k)
 
@@ -474,6 +500,7 @@
             pltpu.VMEM((window, rows, part), BF16),
             pltpu.VMEM((window, rows, part), BF16),
             dma((6,)),
+            pltpu.SemaphoreType.REGULAR,
             dma((2, n)), dma((2, n)),
             dma((n,)), dma((n,)),
             dma((nd,)), dma((nd,)),

time: 19.8 us -> 20.2 us (1.020)
  Pallas kernels: 19 us -> 19.4 us
    pallas_call x1, Pallas kernels: 17.9 us -> 18.3 us  [local(): pl.pallas_call(functools.partial(kernel, sizes), out_shape=shapes, in_spe...]
where the time goes in v4:
time: 20.2 us; the launch traced here: 20.1 us
  Pallas kernels  19.4 us (96%)
  between operations  0.64 us (3%)
    pallas_call x1, Pallas kernels, local(): pl.pallas_call(functools.partial(kernel, sizes), out_shape=shapes, in_spe...  18.3 us
    pallas_call x1, Pallas kernels, local(): pl.pallas_call(write_out, out_shape=shapes, in_specs=[vmem_spec] * 3, out...  1.09 us

profile of v4, /device:TPU:0, one launch (start us, length us, event | category | flops | bytes accessed | tf_op | source)
XLA Modules:
  0.0 20.1 jit_solution(673187540579369584)
XLA Ops:
  0.6 18.3 %packed_attention.1 = (bf16[2048,128]{1,0:T(8,128)(2,1)S(1)}, bf16[2048,128]{1,0:T(8,128)(2,1)S(1)}, bf16[2,256,128]{2,1,0:T(8,128)(2,1)S(1)}) custom-call(bf16[2048,128]{1,0:T(8,128)(2,1)} %bitcast.8, bf16[2,256,128]{2,1,0:T(8,128)(2,1)} %bitcast.10, bf16[2048,128]{1,0:T(8,128)(2,1)} %bitcast.9, s32[1,16]{1,0:T(1,128)} %doc_hbm.1, s32[1,4]{1,0:T(1,128)} %order_hbm.1, ...), custom_call_target="tpu_custom_call" | custom-call | tf_op jit(solution)/shard_map/packed_attention/pallas_call | solution.py:470
  19.0 1.1 %write_out.1 = (bf16[2048,128]{1,0:T(8,128)(2,1)}, bf16[2048,128]{1,0:T(8,128)(2,1)}, bf16[2,256,128]{2,1,0:T(8,128)(2,1)}) custom-call(bf16[2048,128]{1,0:T(8,128)(2,1)S(1)} %get-tuple-element.9.att_ref, bf16[2048,128]{1,0:T(8,128)(2,1)S(1)} %get-tuple-element.10.dq_ref, bf16[2,256,128]{2,1,0:T(8,128)(2,1)S(1)} %get-tuple-element.11.dkv_ref), custom_call_target="tpu_custom_call" | custom-call | tf_op jit(solution)/shard_map/write_out/pallas_call | solution.py:528
